TPU v7x, 128 devices: a whole 4x4x4 slice. The times are simulated.
128 devices in a mesh: pos: 32 (over x, z, core), tile: 4 (over y).
Axes of the slice: x: 4, y: 4, z: 4, core: 2. Of those that a mesh axis runs over, the one named last changes fastest.
Arguments:
- object_field: float32 [2, 2048, 16384], P(None, 'tile', 'pos'), may hold values from -6 to 6
- probe: float32 [2, 256, 256], replicated, may hold values from -45 to 45
- amplitudes: bfloat16 [4, 32, 32, 256, 256], P('tile', 'pos'), may hold values from 0.099609375 to 3
- corner_rows: int32 [4, 32, 32], P('tile', 'pos'), may hold values from 0 to 511, as said below
- corner_cols: int32 [4, 32, 32], P('tile', 'pos'), may hold values from 0 to 511, as said below
- counts: int32 [4, 32], P('tile', 'pos'), may hold values from 1 to 32, as said below
Outputs:
- object_new: float32 [2, 2048, 16384], P(None, 'tile', 'pos')
- probe_grad: float32 [2, 256, 256], replicated
Inputs may be any that keep to these rules, and one draw needn't show every extreme that they name: Slots from counts[t, p] on are unused. `corner_rows`: counted from the first row of the owner's block. `corner_cols`: counted from the first column of the owner's block.
All inputs are finite; a program needn't handle non-finite values.
Results may differ from a plain program's by a relative error of at most 0.0012.
Values sent between devices are 32-bit elements; how exact they have to be, the bound alone decides.
A program may use at most 64 MiB of HBM per device.

v0:
```python
import math

import jax
import jax.numpy as jnp
from jax import lax
from jax.sharding import PartitionSpec as P


def passed_along(block, axis, distance):
    devices = range(lax.axis_size(axis))
    route = [(i - distance, i) for i in devices if i - distance in devices]
    return lax.ppermute(block, axis, route)


def dft_tables(points):
    indices = jnp.arange(points, dtype=jnp.int32)
    residues = indices[:, None] * indices[None, :] % points
    angles = residues.astype(jnp.float32) * (2.0 * math.pi / points)
    factor = 1.0 / math.sqrt(points)
    return (
        (jnp.cos(angles) * factor).astype(jnp.bfloat16),
        (-jnp.sin(angles) * factor).astype(jnp.bfloat16),
    )


def left_batch(table_re, table_im, part_re, part_im):

    def product(matrix, operand):
        return jnp.einsum("jk,bkn->bjn", matrix, operand, preferred_element_type=jnp.float32)

    return (
        product(table_re, part_re) - product(table_im, part_im),
        product(table_re, part_im) + product(table_im, part_re),
    )


def right_batch(part_re, part_im, table_re, table_im):

    def product(operand, matrix):
        return jnp.einsum("bmk,kn->bmn", operand, matrix, preferred_element_type=jnp.float32)

    return (
        product(part_re, table_re) - product(part_im, table_im),
        product(part_re, table_im) + product(part_im, table_re),
    )


def shards(object_field, probe, amplitudes, corner_rows, corner_cols, counts):
    patch_size = probe.shape[1]
    rows_here = object_field.shape[1]
    cols_here = object_field.shape[2]
    slot_total = corner_rows.shape[2]
    group_size = 4
    table_re, table_im = dft_tables(patch_size)
    lower_rim = passed_along(object_field[:, :patch_size, :], "tile", -1)
    tall_block = jnp.concatenate([object_field, lower_rim], axis=1)
    right_rim = passed_along(tall_block[:, :, :patch_size], "pos", -1)
    extended = jnp.concatenate([tall_block, right_rim], axis=2)
    slot_rows = corner_rows.reshape(slot_total)
    slot_cols = corner_cols.reshape(slot_total)
    live_count = counts.reshape(())
    amp_slots = amplitudes.reshape(slot_total, patch_size, patch_size)
    probe_re = probe[0]
    probe_im = probe[1]
    zero_index = jnp.zeros((), jnp.int32)

    def read_patch(row_start, col_start):
        return lax.dynamic_slice(
            extended, (zero_index, row_start, col_start), (2, patch_size, patch_size)
        )

    def compute_group(first_slot):
        rows_sel = lax.dynamic_slice_in_dim(slot_rows, first_slot, group_size)
        cols_sel = lax.dynamic_slice_in_dim(slot_cols, first_slot, group_size)
        patches = jax.vmap(read_patch)(rows_sel, cols_sel)
        amp_sel = lax.dynamic_slice_in_dim(amp_slots, first_slot, group_size, 0)
        slot_ids = first_slot + jnp.arange(group_size, dtype=jnp.int32)
        live_mask = (slot_ids < live_count).astype(jnp.float32)[:, None, None]
        patch_re = patches[:, 0]
        patch_im = patches[:, 1]
        exit_re = probe_re * patch_re - probe_im * patch_im
        exit_im = probe_re * patch_im + probe_im * patch_re
        near_re, near_im = left_batch(
            table_re, table_im, exit_re.astype(jnp.bfloat16), exit_im.astype(jnp.bfloat16)
        )
        far_re, far_im = right_batch(
            near_re.astype(jnp.bfloat16), near_im.astype(jnp.bfloat16), table_re, table_im
        )
        modulus = jnp.sqrt(far_re * far_re + far_im * far_im + 0.25)
        ratio = amp_sel.astype(jnp.float32) / modulus
        back_re, back_im = left_batch(
            table_re,
            -table_im,
            (far_re * ratio).astype(jnp.bfloat16),
            (far_im * ratio).astype(jnp.bfloat16),
        )
        new_re, new_im = right_batch(
            back_re.astype(jnp.bfloat16), back_im.astype(jnp.bfloat16), table_re, -table_im
        )
        delta_re = (new_re - exit_re) * live_mask
        delta_im = (new_im - exit_im) * live_mask
        object_re = probe_re * delta_re + probe_im * delta_im
        object_im = probe_re * delta_im - probe_im * delta_re
        probe_part = jnp.stack(
            [
                jnp.sum(patch_re * delta_re + patch_im * delta_im, axis=0),
                jnp.sum(patch_re * delta_im - patch_im * delta_re, axis=0),
            ]
        )
        return (object_re, object_im, probe_part)

    def group_step(group_index, state):
        update_re, update_im, probe_sum = state
        first_slot = (group_index * group_size).astype(jnp.int32)
        object_re, object_im, probe_part = compute_group(first_slot)
        for member in range(group_size):
            row_start = slot_rows[first_slot + member]
            col_start = slot_cols[first_slot + member]
            current_re = lax.dynamic_slice(
                update_re, (row_start, col_start), (patch_size, patch_size)
            )
            update_re = lax.dynamic_update_slice(
                update_re, current_re + object_re[member], (row_start, col_start)
            )
            current_im = lax.dynamic_slice(
                update_im, (row_start, col_start), (patch_size, patch_size)
            )
            update_im = lax.dynamic_update_slice(
                update_im, current_im + object_im[member], (row_start, col_start)
            )
        return (update_re, update_im, probe_sum + probe_part)

    field_shape = (extended.shape[1], extended.shape[2])
    start_state = (
        jnp.zeros(field_shape, jnp.float32),
        jnp.zeros(field_shape, jnp.float32),
        jnp.zeros((2, patch_size, patch_size), jnp.float32),
    )
    update_re, update_im, probe_sum = lax.fori_loop(
        0, slot_total // group_size, group_step, start_state
    )
    update = jnp.stack([update_re, update_im])
    right_back = passed_along(update[:, :, cols_here:], "pos", 1)
    main_part = update[:, :, :cols_here].at[:, :, :patch_size].add(right_back)
    lower_back = passed_along(main_part[:, rows_here:, :], "tile", 1)
    owned_update = main_part[:, :rows_here, :].at[:, :patch_size, :].add(lower_back)
    probe_total = lax.psum(probe_sum, ("pos", "tile"))
    power = jnp.mean(probe_re * probe_re + probe_im * probe_im) + 1e-06
    object_new = object_field + owned_update / power
    probe_grad = probe_total / math.sqrt(lax.axis_size("pos") * lax.axis_size("tile") * slot_total)
    return (object_new, probe_grad)


def solution(mesh):
    return jax.shard_map(
        shards,
        mesh=mesh,
        in_specs=(
            P(None, "tile", "pos"),
            P(),
            P("tile", "pos", None, None, None),
            P("tile", "pos", None),
            P("tile", "pos", None),
            P("tile", "pos"),
        ),
        out_specs=(P(None, "tile", "pos"), P()),
        check_vma=False,
    )
```

profile of v0, /device:TPU:1, one launch (start us, length us, event | category | flops | bytes accessed | tf_op | source)
XLA Modules:
  0.0 1036.1 jit_solution(14499924393449801990)
XLA Ops:
  10.2 25.0 %collective-permute-done = f32[2,256,512]{2,1,0:T(8,128)S(1)} collective-permute-done((f32[2,256,512]{2,1,0:T(8,128)S(1)}, f32[2,256,512]{2,1,0:T(8,128)S(1)}, u32[]{:S(2)}, u32[]{:S(2)}) %collective-permute-start) | collective-permute-done | bytes 1048608 | tf_op jit(solution)/shard_map/ppermute | solution.py:12
  43.1 18.5 %collective-permute-done.1 = f32[2,768,256]{2,1,0:T(8,128)S(1)} collective-permute-done((f32[2,768,256]{2,1,0:T(8,128)}, f32[2,768,256]{2,1,0:T(8,128)S(1)}, u32[]{:S(2)}, u32[]{:S(2)}) %collective-permute-start.1) | collective-permute-done | bytes 1572896 | tf_op jit(solution)/shard_map/ppermute | solution.py:12
  61.7 4.4 pad_maximum_fusion
  69.3 773.5 %while.28 = (s32[]{:T(128)}, f32[768,768]{1,0:T(8,128)}, f32[768,768]{1,0:T(8,128)}, f32[2,256,256]{2,1,0:T(8,128)}, s32[32]{0:T(128)S(1)}, /*index=5*/s32[32]{0...) while((s32[]{:T(128)}, f32[768,768]{1,0:T(8,128)}, ...), condition=%wide.region_3.4_spmd.clone.clone, body=%wide.region_0.3_spmd.clone.clone.sunk | while | flops 2179465216 | bytes 64488780 | solution.py:139
  69.7 12.4 %while.29 = (s32[]{:T(128)}, f32[2,768,768]{2,1,0:T(8,128)}, s32[4,3]{1,0:T(4,128)S(1)}, f32[4,2,256,256]{3,2,0,1:T(8,128)S(1)}, s32[]{:T(128)}) while((s32[]{:T(128)}, f32[2,768,768]{2,1,0:T(8,128)}, s32[4,3]{1,0:T(4,128)S(1)}, f32[4,2,256,256]{3,2,0,1:T(8,128)S(1)}, s32[]{:T(128)}) %tuple.103), condition=%wide.while_cond.2, body=%wide.while_body.2.sunk | while | flops 2 | bytes 1048693 | solution.py:68
  104.1 4.8 fusion.277
  117.5 3.9 dynamic_update_slice.108
  147.0 3.9 dynamic_update_slice.104
  165.7 12.4 %while.29 = (s32[]{:T(128)}, f32[2,768,768]{2,1,0:T(8,128)}, s32[4,3]{1,0:T(4,128)S(1)}, f32[4,2,256,256]{3,2,0,1:T(8,128)S(1)}, s32[]{:T(128)}) while((s32[]{:T(128)}, f32[2,768,768]{2,1,0:T(8,128)}, s32[4,3]{1,0:T(4,128)S(1)}, f32[4,2,256,256]{3,2,0,1:T(8,128)S(1)}, s32[]{:T(128)}) %tuple.103), condition=%wide.while_cond.2, body=%wide.while_body.2.sunk | while | flops 2 | bytes 1048693 | solution.py:68
  200.2 4.8 fusion.277
  222.3 3.9 dynamic_update_slice.109
  258.3 3.9 dynamic_update_slice.107
  262.5 12.4 %while.29 = (s32[]{:T(128)}, f32[2,768,768]{2,1,0:T(8,128)}, s32[4,3]{1,0:T(4,128)S(1)}, f32[4,2,256,256]{3,2,0,1:T(8,128)S(1)}, s32[]{:T(128)}) while((s32[]{:T(128)}, f32[2,768,768]{2,1,0:T(8,128)}, s32[4,3]{1,0:T(4,128)S(1)}, f32[4,2,256,256]{3,2,0,1:T(8,128)S(1)}, s32[]{:T(128)}) %tuple.103), condition=%wide.while_cond.2, body=%wide.while_body.2.sunk | while | flops 2 | bytes 1048693 | solution.py:68
  297.0 4.8 fusion.277
  310.5 3.9 dynamic_update_slice.108
  319.2 4.0 dynamic_update_slice.109
  359.5 12.4 %while.29 = (s32[]{:T(128)}, f32[2,768,768]{2,1,0:T(8,128)}, s32[4,3]{1,0:T(4,128)S(1)}, f32[4,2,256,256]{3,2,0,1:T(8,128)S(1)}, s32[]{:T(128)}) while((s32[]{:T(128)}, f32[2,768,768]{2,1,0:T(8,128)}, s32[4,3]{1,0:T(4,128)S(1)}, f32[4,2,256,256]{3,2,0,1:T(8,128)S(1)}, s32[]{:T(128)}) %tuple.103), condition=%wide.while_cond.2, body=%wide.while_body.2.sunk | while | flops 2 | bytes 1048693 | solution.py:68
  393.9 4.8 fusion.277
  446.1 4.0 dynamic_update_slice.106
  455.0 12.4 %while.29 = (s32[]{:T(128)}, f32[2,768,768]{2,1,0:T(8,128)}, s32[4,3]{1,0:T(4,128)S(1)}, f32[4,2,256,256]{3,2,0,1:T(8,128)S(1)}, s32[]{:T(128)}) while((s32[]{:T(128)}, f32[2,768,768]{2,1,0:T(8,128)}, s32[4,3]{1,0:T(4,128)S(1)}, f32[4,2,256,256]{3,2,0,1:T(8,128)S(1)}, s32[]{:T(128)}) %tuple.103), condition=%wide.while_cond.2, body=%wide.while_body.2.sunk | while | flops 2 | bytes 1048693 | solution.py:68
  489.5 4.8 fusion.277
  520.4 3.9 dynamic_update_slice.110
  552.2 12.4 %while.29 = (s32[]{:T(128)}, f32[2,768,768]{2,1,0:T(8,128)}, s32[4,3]{1,0:T(4,128)S(1)}, f32[4,2,256,256]{3,2,0,1:T(8,128)S(1)}, s32[]{:T(128)}) while((s32[]{:T(128)}, f32[2,768,768]{2,1,0:T(8,128)}, s32[4,3]{1,0:T(4,128)S(1)}, f32[4,2,256,256]{3,2,0,1:T(8,128)S(1)}, s32[]{:T(128)}) %tuple.103), condition=%wide.while_cond.2, body=%wide.while_body.2.sunk | while | flops 2 | bytes 1048693 | solution.py:68
  586.7 4.8 fusion.277
  649.0 12.4 %while.29 = (s32[]{:T(128)}, f32[2,768,768]{2,1,0:T(8,128)}, s32[4,3]{1,0:T(4,128)S(1)}, f32[4,2,256,256]{3,2,0,1:T(8,128)S(1)}, s32[]{:T(128)}) while((s32[]{:T(128)}, f32[2,768,768]{2,1,0:T(8,128)}, s32[4,3]{1,0:T(4,128)S(1)}, f32[4,2,256,256]{3,2,0,1:T(8,128)S(1)}, s32[]{:T(128)}) %tuple.103), condition=%wide.while_cond.2, body=%wide.while_body.2.sunk | while | flops 2 | bytes 1048693 | solution.py:68
  683.5 4.8 fusion.277
  697.0 4.0 dynamic_update_slice.108
  714.4 3.9 dynamic_update_slice.110
  746.4 12.4 %while.29 = (s32[]{:T(128)}, f32[2,768,768]{2,1,0:T(8,128)}, s32[4,3]{1,0:T(4,128)S(1)}, f32[4,2,256,256]{3,2,0,1:T(8,128)S(1)}, s32[]{:T(128)}) while((s32[]{:T(128)}, f32[2,768,768]{2,1,0:T(8,128)}, s32[4,3]{1,0:T(4,128)S(1)}, f32[4,2,256,256]{3,2,0,1:T(8,128)S(1)}, s32[]{:T(128)}) %tuple.103), condition=%wide.while_cond.2, body=%wide.while_body.2.sunk | while | flops 2 | bytes 1048693 | solution.py:68
  780.9 4.8 fusion.277
  847.9 16.8 %collective-permute-done.2 = f32[2,768,256]{2,1,0:T(8,128)S(1)} collective-permute-done((f32[2,768,256]{2,1,0:T(8,128)S(1)}, f32[2,768,256]{2,1,0:T(8,128)S(1)}, u32[]{:S(2)}, u32[]{:S(2)}) %collective-permute-start.2) | collective-permute-done | bytes 1572896 | tf_op jit(solution)/shard_map/ppermute | solution.py:12
  871.2 150.7 %all-reduce.2.cloned.1.call-done = f32[2,256,256]{2,1,0:T(8,128)} async-done(((f32[2,256,256]{2,1,0:T(8,128)}), f32[2,256,256]{2,1,0:T(8,128)}) %all-reduce.2.cloned.1.call-update) | async-done | bytes 524304 | tf_op jit(solution)/shard_map/psum | solution.py:147
  (471 shorter events, 607.5 us)
Async XLA Ops:
  7.2 2.8 copy-start.5
  7.2 1014.7 %all-reduce.2.cloned.1.call-start = ((), (), s32[]{:S(2)}) async-start(), calls=%async_computation | async-start | bytes 1048576 | tf_op jit(solution)/shard_map/psum | solution.py:147
  8.7 26.5 %collective-permute-start = (f32[2,256,512]{2,1,0:T(8,128)S(1)}, f32[2,256,512]{2,1,0:T(8,128)S(1)}, u32[]{:S(2)}, u32[]{:S(2)}) collective-permute-start(f32[2,256,512]{2,1,0:T(8,128)S(1)} %slice.175), channel_id=1, source_target_pairs={{1,0},{2,1},{3,2},{5,4},{6,5},{7,6},{9,8},{10,9},{11,10},{13,12},{... | collective-permute-start | bytes 3145736 | tf_op jit(solution)/shard_map/ppermute | solution.py:12
  10.2 31.6 %copy-start.7 = (f32[2,256,256]{2,1,0:T(8,128)S(1)}, f32[2,256,256]{2,1,0:T(8,128)}, u32[]{:S(2)}) copy-start(f32[2,256,256]{2,1,0:T(8,128)} %param.13) | copy-start | bytes 1572868
  35.3 1.6 copy-start.4
  38.2 23.5 %collective-permute-start.1 = (f32[2,768,256]{2,1,0:T(8,128)}, f32[2,768,256]{2,1,0:T(8,128)S(1)}, u32[]{:S(2)}, u32[]{:S(2)}) collective-permute-start(f32[2,768,256]{2,1,0:T(8,128)} %slice.227), channel_id=1, source_target_pairs={{4,0},{8,4},{12,8},{16,12},{20,16},{24,20},{28,24},{32,28},{36,32}... | collective-permute-start | bytes 4718600 | tf_op jit(solution)/shard_map/ppermute | solution.py:12
  66.1 3.2 copy-start.8
  66.1 3.2 copy-start.9
  108.9 16.1 %copy-start = (f32[4,256,256]{2,1,0:T(8,128)S(1)}, f32[4,256,256]{2,1,0:T(8,128)}, u32[]{:S(2)}) copy-start(f32[4,256,256]{2,1,0:T(8,128)} %get-tuple-element.669) | copy-start | bytes 3145732 | tf_op jit(solution)/shard_map/while
  205.0 16.1 %copy-start = (f32[4,256,256]{2,1,0:T(8,128)S(1)}, f32[4,256,256]{2,1,0:T(8,128)}, u32[]{:S(2)}) copy-start(f32[4,256,256]{2,1,0:T(8,128)} %get-tuple-element.669) | copy-start | bytes 3145732 | tf_op jit(solution)/shard_map/while
  301.8 16.2 %copy-start = (f32[4,256,256]{2,1,0:T(8,128)S(1)}, f32[4,256,256]{2,1,0:T(8,128)}, u32[]{:S(2)}) copy-start(f32[4,256,256]{2,1,0:T(8,128)} %get-tuple-element.669) | copy-start | bytes 3145732 | tf_op jit(solution)/shard_map/while
  398.7 16.0 %copy-start = (f32[4,256,256]{2,1,0:T(8,128)S(1)}, f32[4,256,256]{2,1,0:T(8,128)}, u32[]{:S(2)}) copy-start(f32[4,256,256]{2,1,0:T(8,128)} %get-tuple-element.669) | copy-start | bytes 3145732 | tf_op jit(solution)/shard_map/while
  494.3 16.2 %copy-start = (f32[4,256,256]{2,1,0:T(8,128)S(1)}, f32[4,256,256]{2,1,0:T(8,128)}, u32[]{:S(2)}) copy-start(f32[4,256,256]{2,1,0:T(8,128)} %get-tuple-element.669) | copy-start | bytes 3145732 | tf_op jit(solution)/shard_map/while
  591.5 16.2 %copy-start = (f32[4,256,256]{2,1,0:T(8,128)S(1)}, f32[4,256,256]{2,1,0:T(8,128)}, u32[]{:S(2)}) copy-start(f32[4,256,256]{2,1,0:T(8,128)} %get-tuple-element.669) | copy-start | bytes 3145732 | tf_op jit(solution)/shard_map/while
  688.3 16.3 %copy-start = (f32[4,256,256]{2,1,0:T(8,128)S(1)}, f32[4,256,256]{2,1,0:T(8,128)}, u32[]{:S(2)}) copy-start(f32[4,256,256]{2,1,0:T(8,128)} %get-tuple-element.669) | copy-start | bytes 3145732 | tf_op jit(solution)/shard_map/while
  785.7 16.1 %copy-start = (f32[4,256,256]{2,1,0:T(8,128)S(1)}, f32[4,256,256]{2,1,0:T(8,128)}, u32[]{:S(2)}) copy-start(f32[4,256,256]{2,1,0:T(8,128)} %get-tuple-element.669) | copy-start | bytes 3145732 | tf_op jit(solution)/shard_map/while
  842.9 4.5 copy-start.1
  842.9 4.5 copy-start.2
  844.5 20.2 %collective-permute-start.2 = (f32[2,768,256]{2,1,0:T(8,128)S(1)}, f32[2,768,256]{2,1,0:T(8,128)S(1)}, u32[]{:S(2)}, u32[]{:S(2)}) collective-permute-start(f32[2,768,256]{2,1,0:T(8,128)S(1)} %pad_maximum_fusion.1), channel_id=1, source_target_pairs={{0,4},{4,8},{8,12},{12,16},{16,20},{20,24},{24,28},{28,32},{32,36}... | collective-permute-start | bytes 4718600 | tf_op jit(solution)/shard_map/ppermute | solution.py:12
  865.0 1.6 copy-start.3
  866.7 158.8 %collective-permute-start.3 = (f32[2,256,512]{2,1,0:T(8,128)S(1)}, f32[2,256,512]{2,1,0:T(8,128)S(1)}, u32[]{:S(2)}, u32[]{:S(2)}) collective-permute-start(f32[2,256,512]{2,1,0:T(8,128)S(1)} %slice.234), channel_id=1, source_target_pairs={{0,1},{1,2},{2,3},{4,5},{5,6},{6,7},{8,9},{9,10},{10,11},{12,13},{... | collective-permute-start | bytes 3145736 | tf_op jit(solution)/shard_map/ppermute | solution.py:12
  1025.5 1.9 copy-start.6
Sparse Core Ops, SparseCore 0:
  870.6 151.2 all-reduce.1
where the time goes:
time: 1050 us; the launch traced here: 1040 us
  local copies, waits for them, and re-layouts  365 us (35%)
  waiting for transfers between devices  211 us (20%)
  matrix products  200 us (19%)
  loops' own time  120 us (11%)
  other arithmetic  113 us (11%)
  between operations  14.9 us (1%)
  starting transfers between devices  11.4 us (1%)
    psum x1, waiting for transfers between devices, shards(): probe_total = lax.psum(probe_sum, ('pos', 'tile'))  151 us
    dynamic_update_slice x32, local copies, waits for them, and re-layouts, group_step(): lax.dynamic_update_slice(update_im, current_im + object_im[member], (row_...  122 us
    dynamic_update_slice x32, local copies, waits for them, and re-layouts, group_step(): lax.dynamic_update_slice(update_re, current_re + object_re[member], (row_...  122 us
    another operation x1, loops' own time, shards(): lax.fori_loop(0, slot_total // group_size, group_step, start_state)  120 us
    dot_general x64, matrix products, product(): jnp.einsum('bmk,kn->bmn', operand, matrix, preferred_element_type=jnp.flo...  119 us
    gather x96, local copies, waits for them, and re-layouts  98.7 us
    dot_general x64, matrix products, product(): jnp.einsum('jk,bkn->bjn', matrix, operand, preferred_element_type=jnp.flo...  80.4 us
    ppermute x4, waiting for transfers between devices, passed_along(): return lax.ppermute(block, axis, route)  60.4 us
  transfers between devices with their start and end apart: 5, of which 4 were waited for; matrix products, arithmetic and copies ran while one was open for 1% of the time, Pallas kernels for 0%

commit v1 on v0

v1 whole, which is shorter than its diff:
```python
import functools

import jax
import jax.numpy as jnp
import ml_dtypes
import numpy as np
from jax import lax
from jax.experimental import pallas as pl
from jax.experimental.pallas import tpu as pltpu
from jax.sharding import PartitionSpec as P

N = 256
H = 128
BLOCK = 512
WIDE = 768


def dft_tables():
    j = np.arange(N)
    angle = (j[:, None] * j[None, :] % N) * (2.0 * np.pi / N)
    re = (np.cos(angle) / np.sqrt(N)).astype(np.float32).astype(ml_dtypes.bfloat16)
    im = (-np.sin(angle) / np.sqrt(N)).astype(np.float32).astype(ml_dtypes.bfloat16)
    return re, im


def stage_tables():
    re, im = dft_tables()

    def pair(a, b, c, d):
        return np.concatenate([np.concatenate([a, b], 1), np.concatenate([c, d], 1)], 0)

    first = [pair(re[:H, q::2], -im[:H, q::2], im[:H, q::2], re[:H, q::2]) for q in (0, 1)]
    second = pair(re, im, -im, re)
    third = [pair(re[q::2, :H], im[q::2, :H], -im[q::2, :H], re[q::2, :H]) for q in (0, 1)]
    fourth = pair(re, -im, im, re)
    return np.stack(first), second, np.stack(third), fourth


def slots_kernel(
    rule, row_base, places,
    rows_ref, cols_ref, count_ref,
    probe_ref, amp_ref, t1_ref, t2_ref, t3_ref, t4_ref, *refs,
):
    n_pieces = len(places)
    pieces = refs[:n_pieces]
    upd_ref, psum_ref = refs[n_pieces : n_pieces + 2]
    (ext, prb_raw, prb, pat, ext_b, exit_s, near_b, fold_b, back_b, amp_buf, order, piece_sem, amp_sem) = refs[n_pieces + 2 :]

    copies = []

    def bring(source, target):
        copies.append(pltpu.make_async_copy(source, target, piece_sem.at[len(copies)]))
        copies[-1].start()

    for b in range(2):
        bring(probe_ref.at[:, :, b * H : (b + 1) * H], prb_raw.at[:, b])
    for piece, (r0, c0) in zip(pieces, places):
        _, h, w = piece.shape
        for b in range(w // H):
            bring(piece.at[:, :, b * H : (b + 1) * H], ext.at[:, c0 // H + b, r0 : r0 + h, :])

    def collect(s, n):
        order[n] = s
        keep = jnp.logical_and(s < count_ref[0, 0], rule(rows_ref[0, 0, s], cols_ref[0, 0, s]))
        return n + keep.astype(jnp.int32)

    total = lax.fori_loop(0, rows_ref.shape[2], collect, jnp.int32(0))

    def amp_copy(i):
        slot = lax.rem(i, 2)
        return pltpu.make_async_copy(amp_ref.at[0, 0, order[i]], amp_buf.at[slot], amp_sem.at[slot])

    @pl.when(total > 0)
    def _():
        amp_copy(0).start()

    upd_ref[...] = jnp.zeros_like(upd_ref)
    psum_ref[...] = jnp.zeros_like(psum_ref)
    for copy in copies:
        copy.wait()
    for comp in range(2):
        for q in range(2):
            for b in range(2):
                prb[comp, q * H : (q + 1) * H, b * H : (b + 1) * H] = prb_raw[comp, b, pl.ds(q, H, stride=2), :]

    lane = lax.broadcasted_iota(jnp.int32, (H, H), 1)

    def step(i, carry):
        s = order[i]
        r = rows_ref[0, 0, s] - row_base
        c = cols_ref[0, 0, s]
        off = lax.rem(c, H)
        c0 = c // H
        back_shift = lax.rem(H - off, H)

        @pl.when(i + 1 < total)
        def _():
            amp_copy(i + 1).start()

        for q in range(2):
            part = []
            for comp in range(2):
                blocks = [
                    pltpu.roll(ext[comp, c0 + b, pl.ds(r + q, H, stride=2), :], back_shift, 1)
                    for b in range(3)
                ]
                part.append(
                    [jnp.where(lane < H - off, blocks[b], blocks[b + 1]) for b in range(2)]
                )
            for b in range(2):
                here = (slice(q * H, (q + 1) * H), slice(b * H, (b + 1) * H))
                pre, pim = prb[0][here], prb[1][here]
                are, aim = part[0][b], part[1][b]
                ere = pre * are - pim * aim
                eim = pre * aim + pim * are
                pat[(0,) + here] = are
                pat[(1,) + here] = aim
                exit_s[(0,) + here] = ere
                exit_s[(1,) + here] = eim
                ext_b[q, 0:H, b * H : (b + 1) * H] = ere.astype(jnp.bfloat16)
                ext_b[q, H:N, b * H : (b + 1) * H] = eim.astype(jnp.bfloat16)

        dot = functools.partial(jnp.dot, preferred_element_type=jnp.float32)
        even = dot(t1_ref[0], ext_b[0])
        odd = dot(t1_ref[1], ext_b[1])
        for comp in range(2):
            e, o = even[comp * H : (comp + 1) * H], odd[comp * H : (comp + 1) * H]
            near_b[0:H, comp * N : (comp + 1) * N] = (e + o).astype(jnp.bfloat16)
            near_b[H:N, comp * N : (comp + 1) * N] = (e - o).astype(jnp.bfloat16)

        amp_copy(i).wait()
        amp = amp_buf.at[lax.rem(i, 2)]
        far = dot(near_b[...], t2_ref[...])
        fre, fim = far[:, :N], far[:, N:]
        ratio = amp[...].astype(jnp.float32) * lax.rsqrt(fre * fre + fim * fim + 0.25)
        for comp, part in enumerate((fre * ratio, fim * ratio)):
            top, low = part[:H], part[H:]
            fold_b[0, comp * H : (comp + 1) * H, :] = (top + low).astype(jnp.bfloat16)
            fold_b[1, comp * H : (comp + 1) * H, :] = (top - low).astype(jnp.bfloat16)

        for q in range(2):
            back = dot(t3_ref[q], fold_b[q])
            for comp in range(2):
                back_b[q * H : (q + 1) * H, comp * N : (comp + 1) * N] = back[comp * H : (comp + 1) * H].astype(
                    jnp.bfloat16
                )
        new = dot(back_b[...], t4_ref[...])
        dre = new[:, :N] - exit_s[0]
        dim = new[:, N:] - exit_s[1]
        psum_ref[0] += pat[0] * dre + pat[1] * dim
        psum_ref[1] += pat[0] * dim - pat[1] * dre
        terms = (prb[0] * dre + prb[1] * dim, prb[0] * dim - prb[1] * dre)
        for comp in range(2):
            for q in range(2):
                z0 = pltpu.roll(terms[comp][q * H : (q + 1) * H, :H], off, 1)
                z1 = pltpu.roll(terms[comp][q * H : (q + 1) * H, H:], off, 1)
                zero = jnp.zeros_like(z0)
                for b, val in enumerate(
                    (jnp.where(lane >= off, z0, zero), jnp.where(lane >= off, z1, z0), jnp.where(lane >= off, zero, z1))
                ):
                    here = (comp, c0 + b, pl.ds(r + q, H, stride=2), slice(None))
                    upd_ref[here] = upd_ref[here] + val
        return carry

    lax.fori_loop(0, total, step, 0)


def run_slots(rule, row_base, height, places, pieces, scalars, probe, amplitudes, tables):
    smem = pl.BlockSpec(memory_space=pltpu.SMEM)
    vmem = pl.BlockSpec(memory_space=pltpu.VMEM)
    hbm = pl.BlockSpec(memory_space=pl.ANY)
    return pl.pallas_call(
        functools.partial(slots_kernel, rule, row_base, places),
        out_shape=(
            jax.ShapeDtypeStruct((2, WIDE // H, height, H), jnp.float32),
            jax.ShapeDtypeStruct((2, N, N), jnp.float32),
        ),
        in_specs=[smem] * 3 + [hbm, hbm] + [vmem] * 4 + [hbm] * len(pieces),
        out_specs=(vmem, vmem),
        scratch_shapes=[
            pltpu.VMEM((2, WIDE // H, height, H), jnp.float32),
            pltpu.VMEM((2, 2, N, H), jnp.float32),
            pltpu.VMEM((2, N, N), jnp.float32),
            pltpu.VMEM((2, N, N), jnp.float32),
            pltpu.VMEM((2, N, N), jnp.bfloat16),
            pltpu.VMEM((2, N, N), jnp.float32),
            pltpu.VMEM((N, 2 * N), jnp.bfloat16),
            pltpu.VMEM((2, N, N), jnp.bfloat16),
            pltpu.VMEM((N, 2 * N), jnp.bfloat16),
            pltpu.VMEM((2, N, N), jnp.bfloat16),
            pltpu.SMEM((40,), jnp.int32),
            pltpu.SemaphoreType.DMA((2 + sum(p.shape[2] // H for p in pieces),)),
            pltpu.SemaphoreType.DMA((2,)),
        ],
        compiler_params=pltpu.CompilerParams(vmem_limit_bytes=40 * 1024 * 1024),
        cost_estimate=pl.CostEstimate(flops=12_000_000_000, bytes_accessed=16_000_000, transcendentals=0),
    )(*scalars, probe, amplitudes, *tables, *pieces)


def passed_along(block, axis, distance):
    devices = range(lax.axis_size(axis))
    route = [(i - distance, i) for i in devices if i - distance in devices]
    return lax.ppermute(block, axis, route)


def interleave(pair):
    return pair.reshape(2, 2, H, N).transpose(0, 2, 1, 3).reshape(2, N, N)


def shards(object_field, probe, amplitudes, corner_rows, corner_cols, counts):
    tables = [jnp.asarray(t) for t in stage_tables()]
    slot_total = corner_rows.shape[2]
    lower = passed_along(object_field[:, :N, :], "tile", -1)
    right = passed_along(object_field[:, :, :N], "pos", -1)
    corner = passed_along(lower[:, :, :N], "pos", -1)
    scalars = (corner_rows, corner_cols, counts)
    upd1, sum1 = run_slots(
        lambda r, c: r <= BLOCK - N, 0, BLOCK, ((0, 0), (0, BLOCK)), (object_field, right),
        scalars, probe, amplitudes, tables,
    )
    upd2, sum2 = run_slots(
        lambda r, c: r > BLOCK - N, N, BLOCK, ((0, 0), (0, BLOCK), (N, 0), (N, BLOCK)),
        (object_field[:, N:, :], right[:, N:, :], lower, corner),
        scalars, probe, amplitudes, tables,
    )
    upd1, upd2 = (u.transpose(0, 2, 1, 3).reshape(2, BLOCK, WIDE) for u in (upd1, upd2))
    update = jnp.pad(upd1, ((0, 0), (0, N), (0, 0))) + jnp.pad(upd2, ((0, 0), (N, 0), (0, 0)))
    right_back = passed_along(update[:, :, BLOCK:], "pos", 1)
    main_part = update[:, :, :BLOCK].at[:, :, :N].add(right_back)
    lower_back = passed_along(main_part[:, BLOCK:, :], "tile", 1)
    owned_update = main_part[:, :BLOCK, :].at[:, :N, :].add(lower_back)
    probe_total = lax.psum(interleave(sum1 + sum2), ("pos", "tile"))
    power = jnp.mean(probe[0] * probe[0] + probe[1] * probe[1]) + 1e-06
    object_new = object_field + owned_update / power
    probe_grad = probe_total / np.sqrt(lax.axis_size("pos") * lax.axis_size("tile") * slot_total).astype(np.float32)
    return (object_new, probe_grad)


def solution(mesh):
    return jax.shard_map(
        shards,
        mesh=mesh,
        in_specs=(
            P(None, "tile", "pos"),
            P(),
            P("tile", "pos", None, None, None),
            P("tile", "pos", None),
            P("tile", "pos", None),
            P("tile", "pos"),
        ),
        out_specs=(P(None, "tile", "pos"), P()),
        check_vma=False,
    )
```

time: 1050 us -> 315 us (0.30); the launches traced: 1040 us -> 314 us
  local copies, waits for them, and re-layouts: 365 us -> 35 us
  matrix products: 200 us -> 0 us
  loops' own time: 120 us -> 0 us
  other arithmetic: 113 us -> 7.39 us
  starting transfers between devices: 11.4 us -> 63.4 us
  waiting for transfers between devices: 211 us -> 182 us
    dynamic_update_slice x64 -> x0, local copies, waits for them, and re-layouts: 243 us -> none  [the longest x32 122 us: group_step(): lax.dynamic_update_slice(update_im, current_im + object_im[member], (row_...]
    dot_general x128 -> x0, matrix products: 200 us -> none  [the longest x64 119 us: product(): jnp.einsum('bmk,kn->bmn', operand, matrix, preferred_element_type=jnp.flo...]
    another operation x9 -> x0, loops' own time: 120 us -> none  [the longest x1 120 us: shards(): lax.fori_loop(0, slot_total // group_size, group_step, start_state)]
    gather x96 -> x0, local copies, waits for them, and re-layouts: 98.7 us -> none
    add x64 -> x3, other arithmetic: 83.2 us -> 2.21 us  [the longest x2 2.15 us: shards(): jnp.pad(upd1, ((0, 0), (0, N), (0, 0)))]
    ppermute x4 -> x5, starting transfers between devices: 11.4 us -> 63.4 us  [passed_along(): return lax.ppermute(block, axis, route)]
    ppermute x4 -> x5, waiting for transfers between devices: 60.4 us -> 38.2 us  [passed_along(): return lax.ppermute(block, axis, route)]
    unnamed x19 -> x60, local copies, waits for them, and re-layouts: 3.76 us -> 19.4 us
  transfers between devices with their start and end apart: 5 -> 6, of which waited for: 4 -> 3; matrix products, arithmetic and copies ran while one was open for 1% -> 4% of each run, Pallas kernels for 0% -> 2%
where the time goes in v1:
time: 315 us; the launch traced here: 314 us
  waiting for transfers between devices  182 us (58%)
  starting transfers between devices  63.4 us (20%)
  local copies, waits for them, and re-layouts  35 us (11%)
  between operations  15.7 us (5%)
  Pallas kernels  10.2 us (3%)
  other arithmetic  7.39 us (2%)
    psum x1, waiting for transfers between devices, shards(): probe_total = lax.psum(interleave(sum1 + sum2), ('pos', 'tile'))  144 us
    ppermute x5, starting transfers between devices, passed_along(): return lax.ppermute(block, axis, route)  63.4 us
    ppermute x5, waiting for transfers between devices, passed_along(): return lax.ppermute(block, axis, route)  38.2 us
    unnamed x60, local copies, waits for them, and re-layouts  19.4 us
    pallas_call x2, Pallas kernels, run_slots(): pl.pallas_call(functools.partial(slots_kernel, rule, row_base, places), o...  10.2 us
    transpose x2, local copies, waits for them, and re-layouts, shards(): u.transpose(0, 2, 1, 3).reshape(2, BLOCK, WIDE)  7.14 us
  transfers between devices with their start and end apart: 6, of which 3 were waited for; matrix products, arithmetic and copies ran while one was open for 4% of the time, Pallas kernels for 2%

profile of v1, /device:TPU:1, one launch (start us, length us, event | category | flops | bytes accessed | tf_op | source)
XLA Modules:
  0.0 314.0 jit_solution(7998359286208367557)
XLA Ops:
  7.2 1.9 fusion.5
  9.2 1.4 collective-permute-start.1
  10.8 3.3 %collective-permute-start = (f32[2,512,256]{2,1,0:T(8,128)S(1)}, f32[2,512,256]{2,1,0:T(8,128)S(1)}, u32[]{:S(2)}, u32[]{:S(2)}) collective-permute-start(f32[2,512,256]{2,1,0:T(8,128)S(1)} %slice.85), channel_id=1, source_target_pairs={{4,0},{8,4},{12,8},{16,12},{20,16},{24,20},{28,24},{32,28},{36,32}... | collective-permute-start | bytes 3145736 | tf_op jit(solution)/shard_map/ppermute | solution.py:203
  14.7 21.2 %collective-permute-done.1.refs_2_ = f32[2,256,512]{2,1,0:T(8,128)S(1)} collective-permute-done((f32[2,256,512]{2,1,0:T(8,128)S(1)}, f32[2,256,512]{2,1,0:T(8,128)S(1)}, u32[]{:S(2)}, u32[]{:S(2)}) %collective-permute-start.1) | collective-permute-done | bytes 1048608 | tf_op jit(solution)/shard_map/ppermute | solution.py:203
  36.8 3.5 %collective-permute-start.2 = (f32[2,256,256]{2,1,0:T(8,128)}, f32[2,256,256]{2,1,0:T(8,128)}, u32[]{:S(2)}, u32[]{:S(2)}) collective-permute-start(f32[2,256,256]{2,1,0:T(8,128)} %slice.99), channel_id=1, source_target_pairs={{4,0},{8,4},{12,8},{16,12},{20,16},{24,20},{28,24},{32,28},{36,32}... | collective-permute-start | bytes 1572872 | tf_op jit(solution)/shard_map/ppermute | solution.py:203
  40.4 1.0 copy-done.19
  41.4 0.9 copy-done.21
  42.3 0.9 copy-done.23
  43.3 6.6 %shard_map.113 = (f32[2,6,512,128]{3,2,1,0:T(8,128)S(1)}, f32[2,256,256]{2,1,0:T(8,128)S(1)}) custom-call(s32[1,1,32]{2,1,0:T(1,128)S(1)} %copy-done.15, s32[1,1,32]{2,1,0:T(1,128)S(1)} %copy-done.16, s32[1,1]{1,0:T(1,128)S(6)} %copy.21.count_ref, f32[2,256,256]{2,1,0:T(8,128)S(1)} %copy-done.7, bf16[1,1,32,256,256]{4,3,2,1,0:T(8,128)(2,1)S(1)} %copy-done.13, ...), custom_call_target="tpu_custom_call" | custom-call | flops 12000000000 | bytes 16000000 | tf_op jit(solution)/shard_map/pallas_call | solution.py:172
  49.9 1.7 copy-done.2
  52.4 3.6 %copy.13 = f32[2,512,6,128]{1,3,2,0:T(8,128)} copy(f32[2,512,6,128]{3,1,2,0:T(8,128)} %bitcast.8) | data formatting | bytes 6291456 | tf_op jit(solution)/shard_map/transpose | solution.py:226
  55.9 1.1 slice.98.refs_1_
  57.0 1.0 copy-done.8
  58.1 1.2 copy-done.11
  59.3 2.2 copy-done.14
  61.5 1.0 copy-done.18
  62.5 1.0 copy-done.20
  64.5 3.6 %shard_map.114 = (f32[2,6,512,128]{3,2,1,0:T(8,128)S(1)}, f32[2,256,256]{2,1,0:T(8,128)S(1)}) custom-call(s32[1,1,32]{2,1,0:T(1,128)S(1)} %copy-done.15, s32[1,1,32]{2,1,0:T(1,128)S(1)} %copy-done.16, s32[1,1]{1,0:T(1,128)S(6)} %copy.21.count_ref, f32[2,256,256]{2,1,0:T(8,128)S(1)} %copy-done.8, bf16[1,1,32,256,256]{4,3,2,1,0:T(8,128)(2,1)S(1)} %copy-done.14, ...), custom_call_target="tpu_custom_call" | custom-call | flops 12000000000 | bytes 16000000 | tf_op jit(solution)/shard_map/pallas_call | solution.py:172
  68.2 1.7 copy-done.1
  70.7 3.6 %copy.14 = f32[2,512,6,128]{1,3,2,0:T(8,128)} copy(f32[2,512,6,128]{3,1,2,0:T(8,128)} %bitcast.7) | data formatting | bytes 6291456 | tf_op jit(solution)/shard_map/transpose | solution.py:226
  74.3 1.8 pad_add_fusion
  76.1 51.0 %collective-permute-start.3 = (f32[2,768,256]{1,2,0:T(8,128)S(1)}, f32[2,768,256]{1,2,0:T(8,128)S(1)}, u32[]{:S(2)}, u32[]{:S(2)}) collective-permute-start(f32[2,768,256]{1,2,0:T(8,128)S(1)} %pad_add_fusion), channel_id=1, source_target_pairs={{0,4},{4,8},{8,12},{12,16},{16,20},{20,24},{24,28},{28,32},{32,36}... | collective-permute-start | bytes 4718600 | tf_op jit(solution)/shard_map/ppermute | solution.py:203
  127.5 17.0 %collective-permute-done.3 = f32[2,768,256]{1,2,0:T(8,128)S(1)} collective-permute-done((f32[2,768,256]{1,2,0:T(8,128)S(1)}, f32[2,768,256]{1,2,0:T(8,128)S(1)}, u32[]{:S(2)}, u32[]{:S(2)}) %collective-permute-start.3) | collective-permute-done | bytes 1572896 | tf_op jit(solution)/shard_map/ppermute | solution.py:203
  144.8 1.1 slice.106
  145.9 4.2 %collective-permute-start.4 = (f32[2,256,512]{1,2,0:T(8,128)}, f32[2,256,512]{1,2,0:T(8,128)}, u32[]{:S(2)}, u32[]{:S(2)}) collective-permute-start(f32[2,256,512]{1,2,0:T(8,128)} %slice.106), channel_id=1, source_target_pairs={{0,1},{1,2},{2,3},{4,5},{5,6},{6,7},{8,9},{9,10},{10,11},{12,13},{... | collective-permute-start | bytes 3145736 | tf_op jit(solution)/shard_map/ppermute | solution.py:203
  150.6 1.2 reshape.83
  151.7 1.8 copy.15
  154.9 144.1 %all-reduce.4.cloned.1.call-done = f32[2,256,256]{2,1,0:T(8,128)} async-done(((f32[2,256,256]{2,1,0:T(8,128)}), f32[2,256,256]{2,1,0:T(8,128)}) %all-reduce.4.cloned.1.call-update) | async-done | bytes 524304 | tf_op jit(solution)/shard_map/psum | solution.py:232
  299.0 1.9 broadcast_multiply_fusion
  300.8 1.8 slice.104
  302.6 1.9 fusion.4
  305.3 1.8 copy.17
  (61 shorter events, 6.2 us)
Async XLA Ops:
  7.2 3.5 %copy-start = (f32[2,512,512]{2,1,0:T(8,128)S(1)}, f32[2,512,512]{2,1,0:T(8,128)}, u32[]{:S(2)}) copy-start(f32[2,512,512]{2,1,0:T(8,128)} %refs_0_.1) | copy-start | bytes 6291460
  7.2 291.8 %all-reduce.4.cloned.1.call-start = ((), (), s32[]{:S(2)}) async-start(), calls=%async_computation | async-start | bytes 1048576 | tf_op jit(solution)/shard_map/psum | solution.py:232
  7.2 33.1 %copy-start.13 = (bf16[1,1,32,256,256]{4,3,2,1,0:T(8,128)(2,1)S(1)}, bf16[1,1,32,256,256]{4,3,2,1,0:T(8,128)(2,1)}, u32[]{:S(2)}) copy-start(bf16[1,1,32,256,256]{4,3,2,1,0:T(8,128)(2,1)} %amp_ref.3) | copy-start | bytes 12582916
  9.2 31.1 %copy-start.7 = (f32[2,256,256]{2,1,0:T(8,128)S(1)}, f32[2,256,256]{2,1,0:T(8,128)}, u32[]{:S(2)}) copy-start(f32[2,256,256]{2,1,0:T(8,128)} %probe_ref.3) | copy-start | bytes 1572868
  9.2 31.1 %copy-start.15 = (s32[1,1,32]{2,1,0:T(1,128)S(1)}, s32[1,1,32]{2,1,0:T(1,128)}, u32[]{:S(2)}) copy-start(s32[1,1,32]{2,1,0:T(1,128)} %rows_ref.3) | copy-start | bytes 388
  9.2 31.1 %copy-start.16 = (s32[1,1,32]{2,1,0:T(1,128)S(1)}, s32[1,1,32]{2,1,0:T(1,128)}, u32[]{:S(2)}) copy-start(s32[1,1,32]{2,1,0:T(1,128)} %cols_ref.3) | copy-start | bytes 388
  9.2 31.1 %copy-start.17 = (bf16[512,512]{1,0:T(8,128)(2,1)S(1)}, bf16[512,512]{1,0:T(8,128)(2,1)}, u32[]{:S(2)}) copy-start(bf16[512,512]{1,0:T(8,128)(2,1)} %constant.73.clone.t2_ref) | copy-start | bytes 1572868
  9.2 26.7 %collective-permute-start.1 = (f32[2,256,512]{2,1,0:T(8,128)S(1)}, f32[2,256,512]{2,1,0:T(8,128)S(1)}, u32[]{:S(2)}, u32[]{:S(2)}) collective-permute-start(f32[2,256,512]{2,1,0:T(8,128)S(1)} %get-tuple-element.36), channel_id=1, source_target_pairs={{1,0},{2,1},{3,2},{5,4},{6,5},{7,6},{9,8},{10,9},{11,10},{13,12},{... | collective-permute-start | bytes 3145736 | tf_op jit(solution)/shard_map/ppermute | solution.py:203
  10.8 29.5 %collective-permute-start = (f32[2,512,256]{2,1,0:T(8,128)S(1)}, f32[2,512,256]{2,1,0:T(8,128)S(1)}, u32[]{:S(2)}, u32[]{:S(2)}) collective-permute-start(f32[2,512,256]{2,1,0:T(8,128)S(1)} %slice.85), channel_id=1, source_target_pairs={{4,0},{8,4},{12,8},{16,12},{20,16},{24,20},{28,24},{32,28},{36,32}... | collective-permute-start | bytes 3145736 | tf_op jit(solution)/shard_map/ppermute | solution.py:203
  35.9 4.4 %copy-start.10 = (f32[2,256,512]{2,1,0:T(8,128)}, f32[2,256,512]{2,1,0:T(8,128)S(1)}, u32[]{:S(2)}) copy-start(f32[2,256,512]{2,1,0:T(8,128)S(1)} %collective-permute-done.1.refs_2_) | copy-start | bytes 3145732
  36.8 20.2 %collective-permute-start.2 = (f32[2,256,256]{2,1,0:T(8,128)}, f32[2,256,256]{2,1,0:T(8,128)}, u32[]{:S(2)}, u32[]{:S(2)}) collective-permute-start(f32[2,256,256]{2,1,0:T(8,128)} %slice.99), channel_id=1, source_target_pairs={{4,0},{8,4},{12,8},{16,12},{20,16},{24,20},{28,24},{32,28},{36,32}... | collective-permute-start | bytes 1572872 | tf_op jit(solution)/shard_map/ppermute | solution.py:203
  40.3 1.0 copy-start.19
  41.4 0.9 copy-start.21
  42.3 0.9 copy-start.23
  43.3 6.6 %copy-start.12 = (f32[2,512,256]{2,1,0:T(8,128)}, f32[2,512,256]{2,1,0:T(8,128)S(1)}, u32[]{:S(2)}) copy-start(f32[2,512,256]{2,1,0:T(8,128)S(1)} %collective-permute-done.refs_1_) | copy-start | bytes 3145732
  49.9 1.7 copy-start.2
  52.4 4.7 %copy-start.22 = (bf16[2,256,256]{2,1,0:T(8,128)(2,1)S(1)}, bf16[2,256,256]{2,1,0:T(8,128)(2,1)}, u32[]{:S(2)}) copy-start(bf16[2,256,256]{2,1,0:T(8,128)(2,1)} %constant.72.clone.t1_ref) | copy-start | bytes 786436
  57.0 1.0 copy-start.8
  58.1 1.2 copy-start.11
  59.3 2.2 copy-start.14
  61.5 1.0 copy-start.18
  62.5 1.0 copy-start.20
  68.2 1.7 copy-start.1
  74.3 52.9 %copy-start.25 = (f32[2,512,6,128]{1,3,2,0:T(8,128)S(1)}, f32[2,512,6,128]{1,3,2,0:T(8,128)}, u32[]{:S(2)}) copy-start(f32[2,512,6,128]{1,3,2,0:T(8,128)} %copy.13) | copy-start | bytes 9437188
  74.3 52.9 %copy-start.26 = (f32[2,512,6,128]{1,3,2,0:T(8,128)S(1)}, f32[2,512,6,128]{1,3,2,0:T(8,128)}, u32[]{:S(2)}) copy-start(f32[2,512,6,128]{1,3,2,0:T(8,128)} %copy.14) | copy-start | bytes 9437188
  76.1 68.4 %collective-permute-start.3 = (f32[2,768,256]{1,2,0:T(8,128)S(1)}, f32[2,768,256]{1,2,0:T(8,128)S(1)}, u32[]{:S(2)}, u32[]{:S(2)}) collective-permute-start(f32[2,768,256]{1,2,0:T(8,128)S(1)} %pad_add_fusion), channel_id=1, source_target_pairs={{0,4},{4,8},{8,12},{12,16},{16,20},{20,24},{24,28},{28,32},{32,36}... | collective-permute-start | bytes 4718600 | tf_op jit(solution)/shard_map/ppermute | solution.py:203
  144.8 5.4 %copy-start.27 = (f32[2,768,512]{1,2,0:T(8,128)}, f32[2,768,512]{1,2,0:T(8,128)S(1)}, u32[]{:S(2)}) copy-start(f32[2,768,512]{1,2,0:T(8,128)S(1)} %fusion.3) | copy-start | bytes 9437188
  144.8 5.3 %copy-start.4 = (f32[2,256,256]{2,1,0:T(8,128)S(1)}, f32[2,256,256]{2,1,0:T(8,128)}, u32[]{:S(2)}) copy-start(f32[2,256,256]{2,1,0:T(8,128)} %copy-done.3) | copy-start | bytes 1572868
  144.8 5.3 %copy-start.6 = (f32[2,256,256]{2,1,0:T(8,128)S(1)}, f32[2,256,256]{2,1,0:T(8,128)}, u32[]{:S(2)}) copy-start(f32[2,256,256]{2,1,0:T(8,128)} %copy-done.5) | copy-start | bytes 1572868
  145.9 156.7 %collective-permute-start.4 = (f32[2,256,512]{1,2,0:T(8,128)}, f32[2,256,512]{1,2,0:T(8,128)}, u32[]{:S(2)}, u32[]{:S(2)}) collective-permute-start(f32[2,256,512]{1,2,0:T(8,128)} %slice.106), channel_id=1, source_target_pairs={{0,1},{1,2},{2,3},{4,5},{5,6},{6,7},{8,9},{9,10},{10,11},{12,13},{... | collective-permute-start | bytes 3145736 | tf_op jit(solution)/shard_map/ppermute | solution.py:203
  151.7 1.8 copy-start.9
  302.6 2.2 copy-start.28
  (3 other events, 2.5 us)
Sparse Core Ops, SparseCore 0:
  151.9 147.0 all-reduce.3

commit v2 on v1

--- a/solution.py
+++ b/solution.py
@@ -1,4 +1,5 @@
 import functools
+import math
 
 import jax
 import jax.numpy as jnp
@@ -37,14 +38,18 @@
 
 
 def slots_kernel(
-    rule, row_base, places,
+    rule, row_base, places, follows,
     rows_ref, cols_ref, count_ref,
     probe_ref, amp_ref, t1_ref, t2_ref, t3_ref, t4_ref, *refs,
 ):
     n_pieces = len(places)
     pieces = refs[:n_pieces]
-    upd_ref, psum_ref = refs[n_pieces : n_pieces + 2]
-    (ext, prb_raw, prb, pat, ext_b, exit_s, near_b, fold_b, back_b, amp_buf, order, piece_sem, amp_sem) = refs[n_pieces + 2 :]
+    refs = refs[n_pieces:]
+    if follows:
+        before = refs[:2]
+        refs = refs[2:]
+    upd_ref, psum_ref = refs[:2]
+    (ext, prb_raw, prb, pat, ext_b, exit_s, near_b, fold_b, back_b, amp_buf, order, piece_sem, amp_sem) = refs[2:]
 
     copies = []
 
@@ -74,8 +79,13 @@
     def _():
         amp_copy(0).start()
 
-    upd_ref[...] = jnp.zeros_like(upd_ref)
-    psum_ref[...] = jnp.zeros_like(psum_ref)
+    if follows:
+        bring(before[0].at[:, :, N:, :], upd_ref.at[:, :, :N, :])
+        bring(before[1], psum_ref)
+        upd_ref[:, :, N:, :] = jnp.zeros((2, WIDE // H, N, H), jnp.float32)
+    else:
+        upd_ref[...] = jnp.zeros_like(upd_ref)
+        psum_ref[...] = jnp.zeros_like(psum_ref)
     for copy in copies:
         copy.wait()
     for comp in range(2):
@@ -163,19 +173,26 @@
         return carry
 
     lax.fori_loop(0, total, step, 0)
-
-
-def run_slots(rule, row_base, height, places, pieces, scalars, probe, amplitudes, tables):
+    if follows:
+        for comp in range(2):
+            for b in range(2):
+                lanes = slice(b * H, (b + 1) * H)
+                for q in range(2):
+                    prb_raw[comp, b, pl.ds(q, H, stride=2), :] = psum_ref[comp, q * H : (q + 1) * H, lanes]
+                psum_ref[comp, :, lanes] = prb_raw[comp, b]
+
+
+def run_slots(rule, row_base, height, places, pieces, before, scalars, probe, amplitudes, tables):
     smem = pl.BlockSpec(memory_space=pltpu.SMEM)
     vmem = pl.BlockSpec(memory_space=pltpu.VMEM)
     hbm = pl.BlockSpec(memory_space=pl.ANY)
     return pl.pallas_call(
-        functools.partial(slots_kernel, rule, row_base, places),
+        functools.partial(slots_kernel, rule, row_base, places, bool(before)),
         out_shape=(
             jax.ShapeDtypeStruct((2, WIDE // H, height, H), jnp.float32),
             jax.ShapeDtypeStruct((2, N, N), jnp.float32),
         ),
-        in_specs=[smem] * 3 + [hbm, hbm] + [vmem] * 4 + [hbm] * len(pieces),
+        in_specs=[smem] * 3 + [hbm, hbm] + [vmem] * 4 + [hbm] * (len(pieces) + len(before)),
         out_specs=(vmem, vmem),
         scratch_shapes=[
             pltpu.VMEM((2, WIDE // H, height, H), jnp.float32),
@@ -189,12 +206,12 @@
             pltpu.VMEM((N, 2 * N), jnp.bfloat16),
             pltpu.VMEM((2, N, N), jnp.bfloat16),
             pltpu.SMEM((40,), jnp.int32),
-            pltpu.SemaphoreType.DMA((2 + sum(p.shape[2] // H for p in pieces),)),
+            pltpu.SemaphoreType.DMA((4 + sum(p.shape[2] // H for p in pieces),)),
             pltpu.SemaphoreType.DMA((2,)),
         ],
         compiler_params=pltpu.CompilerParams(vmem_limit_bytes=40 * 1024 * 1024),
         cost_estimate=pl.CostEstimate(flops=12_000_000_000, bytes_accessed=16_000_000, transcendentals=0),
-    )(*scalars, probe, amplitudes, *tables, *pieces)
+    )(*scalars, probe, amplitudes, *tables, *pieces, *before)
 
 
 def passed_along(block, axis, distance):
@@ -203,37 +220,176 @@
     return lax.ppermute(block, axis, route)
 
 
-def interleave(pair):
-    return pair.reshape(2, 2, H, N).transpose(0, 2, 1, 3).reshape(2, N, N)
+def exchange_kernel(
+    first_ref, second_ref, obj_ref, sum_ref, probe_ref, out_ref, grad_ref,
+    from_left, from_above, corner, pair_in, part, x_in, piece, tile_in, gathered,
+    right_send, right_recv, low_send, low_recv, pair_send, pair_recv, x_send, x_recv,
+    t_send, t_recv, tg_send, tg_recv, xg_send, xg_recv, cg_send, cg_recv,
+):
+    p = lax.axis_index("pos")
+    t = lax.axis_index("tile")
+    x, z, core = p // 8, (p // 2) % 4, p % 2
+    g = z * 4 + t
+
+    def pos_of(xx, zz, cc):
+        return xx * 8 + zz * 2 + cc
+
+    right = {"pos": (p + 1) % 32, "tile": t}
+    left = {"pos": (p + 31) % 32, "tile": t}
+    below = {"pos": p, "tile": (t + 1) % 4}
+    partner = {"pos": pos_of(x, z, 1 - core), "tile": t}
+    x_peers = [{"pos": pos_of((x + d) % 4, z, core), "tile": t} for d in (1, 2, 3)]
+    g_peers = [{"pos": pos_of(x, ((g + d) % 16) // 4, core), "tile": (g + d) % 4} for d in range(1, 16)]
+
+    barrier = pltpu.get_barrier_semaphore()
+    for peer in [right, left, partner] + x_peers + g_peers:
+        pl.semaphore_signal(barrier, inc=1, device_id=peer, device_id_type=pl.DeviceIdType.MESH)
+    pl.semaphore_wait(barrier, 21)
+
+    started = []
+
+    def send(source, target, send_sem, recv_sem, peer):
+        copy = pltpu.make_async_remote_copy(
+            src_ref=source, dst_ref=target, send_sem=send_sem, recv_sem=recv_sem,
+            device_id=peer, device_id_type=pl.DeviceIdType.MESH,
+        )
+        copy.start()
+        started.append(copy)
+        return copy
+
+    edge = send(second_ref.at[:, 4:6, N:, :], from_left.at[:, :, 2 * N :, :], right_send.at[0], right_recv.at[0], right)
+    low1 = send(second_ref.at[:, 2:4, N:, :], from_above.at[:, 2:4], low_send.at[0], low_recv.at[0], below)
+    half = send(sum_ref.at[pl.ds((1 - core) * N, N)], pair_in, pair_send.at[0], pair_recv.at[0], partner)
+    mid = send(second_ref.at[:, 4:6, :N, :], from_left.at[:, :, N : 2 * N, :], right_send.at[1], right_recv.at[1], right)
+    top = send(first_ref.at[:, 4:6, :N, :], from_left.at[:, :, :N, :], right_send.at[2], right_recv.at[2], right)
+
+    half.wait_recv()
+    part[...] = sum_ref[pl.ds(core * N, N), :] + pair_in[...]
+    x_copies = [
+        send(part.at[pl.ds(((x + d) % 4) * 64, 64)], x_in.at[d - 1], x_send.at[d - 1], x_recv.at[d - 1], x_peers[d - 1])
+        for d in (1, 2, 3)
+    ]
+
+    edge.wait_recv()
+    has_left = (p > 0).astype(jnp.float32)
+    has_above = (t > 0).astype(jnp.float32)
+    corner[...] = second_ref[:, 0:2, N:, :] + from_left[:, :, 2 * N :, :] * has_left
+    low0 = send(corner, from_above.at[:, 0:2], low_send.at[1], low_recv.at[1], below)
+
+    for copy in x_copies:
+        copy.wait_recv()
+    shard = part[pl.ds(x * 64, 64), :] + x_in[0] + x_in[1] + x_in[2]
+    for rg in range(8):
+        for lg in range(2):
+            piece[rg * 2 + lg] = shard[rg * 8 : rg * 8 + 8, lg * H : (lg + 1) * H]
+    t_copies = [
+        send(piece.at[(g + d) % 16], tile_in.at[d - 1], t_send.at[d - 1], t_recv.at[d - 1], g_peers[d - 1])
+        for d in range(1, 16)
+    ]
+    power = jnp.sum(probe_ref[...] * probe_ref[...]) * (1.0 / (N * N)) + 1e-06
+    scale = 1.0 / jnp.full((1, H), power, jnp.float32)
+
+    for copy in t_copies:
+        copy.wait_recv()
+    own = piece[g]
+    for d in range(15):
+        own = own + tile_in[d]
+    slots = 128 * 32
+    gathered[core, x, g] = own * np.float32(1.0 / math.sqrt(slots))
+    tg_copies = [
+        send(gathered.at[core, x, g], gathered.at[core, x, g], tg_send.at[d - 1], tg_recv.at[d - 1], g_peers[d - 1])
+        for d in range(1, 16)
+    ]
+
+    for copy in tg_copies:
+        copy.wait_recv()
+    xg_copies = [
+        send(gathered.at[core, x], gathered.at[core, x], xg_send.at[d - 1], xg_recv.at[d - 1], x_peers[d - 1])
+        for d in (1, 2, 3)
+    ]
+    cg_copies = [send(gathered.at[core, x], gathered.at[core, x], cg_send.at[0], cg_recv.at[0], partner)]
+
+    def put(b, r0, value):
+        for comp in range(2):
+            here = (comp, slice(r0, r0 + N), slice(b * H, (b + 1) * H))
+            out_ref[here] = obj_ref[here] + value[comp] * scale
+
+    for b in (2, 3):
+        put(b, N, second_ref[:, b, :N, :])
+    for d in (1, 2, 3):
+        xg_copies[d - 1].wait_recv()
+        came = (x + 4 - d) % 4
+        cg_copies.append(
+            send(gathered.at[core, came], gathered.at[core, came], cg_send.at[d], cg_recv.at[d], partner)
+        )
+    mid.wait_recv()
+    for b in (0, 1):
+        put(b, N, second_ref[:, b, :N, :] + from_left[:, b, N : 2 * N, :] * has_left)
+    low1.wait_recv()
+    for b in (2, 3):
+        put(b, 0, first_ref[:, b, :N, :] + from_above[:, b] * has_above)
+    top.wait_recv()
+    for copy in cg_copies:
+        copy.wait_recv()
+    for h in range(2):
+        for xx in range(4):
+            for rg in range(8):
+                for lg in range(2):
+                    grad_ref[h, xx * 64 + rg * 8 : xx * 64 + rg * 8 + 8, lg * H : (lg + 1) * H] = gathered[h, xx, rg * 2 + lg]
+    low0.wait_recv()
+    for b in (0, 1):
+        put(b, 0, first_ref[:, b, :N, :] + from_left[:, b, :N, :] * has_left + from_above[:, b] * has_above)
+    for copy in started:
+        copy.wait_send()
+
+
+def exchange(first, second, object_field, total, probe):
+    vmem = pl.BlockSpec(memory_space=pltpu.VMEM)
+    f32 = jnp.float32
+    dma = pltpu.SemaphoreType.DMA
+    return pl.pallas_call(
+        exchange_kernel,
+        out_shape=(
+            jax.ShapeDtypeStruct((2, BLOCK, BLOCK), f32),
+            jax.ShapeDtypeStruct((2, N, N), f32),
+        ),
+        in_specs=[vmem] * 5,
+        out_specs=(vmem, vmem),
+        scratch_shapes=[
+            pltpu.VMEM((2, 2, WIDE, H), f32),
+            pltpu.VMEM((2, 4, N, H), f32),
+            pltpu.VMEM((2, 2, N, H), f32),
+            pltpu.VMEM((N, N), f32),
+            pltpu.VMEM((N, N), f32),
+            pltpu.VMEM((3, 64, N), f32),
+            pltpu.VMEM((16, 8, H), f32),
+            pltpu.VMEM((15, 8, H), f32),
+            pltpu.VMEM((2, 4, 16, 8, H), f32),
+            dma((3,)), dma((3,)), dma((2,)), dma((2,)), dma((1,)), dma((1,)), dma((3,)), dma((3,)),
+            dma((15,)), dma((15,)), dma((15,)), dma((15,)), dma((3,)), dma((3,)), dma((4,)), dma((4,)),
+        ],
+        compiler_params=pltpu.CompilerParams(
+            collective_id=0, has_side_effects=True, vmem_limit_bytes=32 * 1024 * 1024
+        ),
+    )(first, second, object_field, total, probe)
 
 
 def shards(object_field, probe, amplitudes, corner_rows, corner_cols, counts):
     tables = [jnp.asarray(t) for t in stage_tables()]
-    slot_total = corner_rows.shape[2]
     lower = passed_along(object_field[:, :N, :], "tile", -1)
     right = passed_along(object_field[:, :, :N], "pos", -1)
     corner = passed_along(lower[:, :, :N], "pos", -1)
     scalars = (corner_rows, corner_cols, counts)
     upd1, sum1 = run_slots(
-        lambda r, c: r <= BLOCK - N, 0, BLOCK, ((0, 0), (0, BLOCK)), (object_field, right),
+        lambda r, c: r <= BLOCK - N, 0, BLOCK, ((0, 0), (0, BLOCK)), (object_field, right), (),
         scalars, probe, amplitudes, tables,
     )
     upd2, sum2 = run_slots(
         lambda r, c: r > BLOCK - N, N, BLOCK, ((0, 0), (0, BLOCK), (N, 0), (N, BLOCK)),
-        (object_field[:, N:, :], right[:, N:, :], lower, corner),
+        (object_field[:, N:, :], right[:, N:, :], lower, corner), (upd1, sum1),
         scalars, probe, amplitudes, tables,
     )
-    upd1, upd2 = (u.transpose(0, 2, 1, 3).reshape(2, BLOCK, WIDE) for u in (upd1, upd2))
-    update = jnp.pad(upd1, ((0, 0), (0, N), (0, 0))) + jnp.pad(upd2, ((0, 0), (N, 0), (0, 0)))
-    right_back = passed_along(update[:, :, BLOCK:], "pos", 1)
-    main_part = update[:, :, :BLOCK].at[:, :, :N].add(right_back)
-    lower_back = passed_along(main_part[:, BLOCK:, :], "tile", 1)
-    owned_update = main_part[:, :BLOCK, :].at[:, :N, :].add(lower_back)
-    probe_total = lax.psum(interleave(sum1 + sum2), ("pos", "tile"))
-    power = jnp.mean(probe[0] * probe[0] + probe[1] * probe[1]) + 1e-06
-    object_new = object_field + owned_update / power
-    probe_grad = probe_total / np.sqrt(lax.axis_size("pos") * lax.axis_size("tile") * slot_total).astype(np.float32)
-    return (object_new, probe_grad)
+    return exchange(upd1, upd2, object_field, sum2.reshape(2 * N, N), probe)
 
 
 def solution(mesh):

time: 315 us -> 140 us (0.44)
  waiting for transfers between devices: 182 us -> 21.2 us
  Pallas kernels: 10.2 us -> 101 us
  starting transfers between devices: 63.4 us -> 8.33 us
  local copies, waits for them, and re-layouts: 35 us -> 7.14 us
  between operations: 15.7 us -> 1.5 us
  other arithmetic: 7.39 us -> 0 us
    psum x1 -> x0, waiting for transfers between devices: 144 us -> none  [shards(): probe_total = lax.psum(interleave(sum1 + sum2), ('pos', 'tile'))]
    pallas_call x2 -> x3, Pallas kernels: 10.2 us -> 101 us  [the longest x1 72.3 us: exchange(): pl.pallas_call(exchange_kernel, out_shape=(jax.ShapeDtypeStruct((2, BLOCK...]
    ppermute x5 -> x3, starting transfers between devices: 63.4 us -> 8.33 us  [passed_along(): return lax.ppermute(block, axis, route)]
    ppermute x5 -> x3, waiting for transfers between devices: 38.2 us -> 21.2 us  [passed_along(): return lax.ppermute(block, axis, route)]
    unnamed x60 -> x26, local copies, waits for them, and re-layouts: 19.4 us -> 5.1 us
    transpose x3 -> x0, local copies, waits for them, and re-layouts: 7.54 us -> none  [the longest x2 7.14 us: shards(): u.transpose(0, 2, 1, 3).reshape(2, BLOCK, WIDE)]
  transfers between devices with their start and end apart: 6 -> 3, of which waited for: 3 -> 1; matrix products, arithmetic and copies ran while one was open for 4% -> 0% of each run, Pallas kernels for 2% -> 7%
where the time goes in v2:
time: 140 us; the launch traced here: 139 us
  Pallas kernels  101 us (72%)
  waiting for transfers between devices  21.2 us (15%)
  starting transfers between devices  8.33 us (6%)
  local copies, waits for them, and re-layouts  7.14 us (5%)
  between operations  1.5 us (1%)
    pallas_call x1, Pallas kernels, exchange(): pl.pallas_call(exchange_kernel, out_shape=(jax.ShapeDtypeStruct((2, BLOCK...  72.3 us
    pallas_call x2, Pallas kernels, run_slots(): pl.pallas_call(functools.partial(slots_kernel, rule, row_base, places, bo...  29 us
    ppermute x3, waiting for transfers between devices, passed_along(): return lax.ppermute(block, axis, route)  21.2 us
    ppermute x3, starting transfers between devices, passed_along(): return lax.ppermute(block, axis, route)  8.33 us
    unnamed x26, local copies, waits for them, and re-layouts  5.1 us
  transfers between devices with their start and end apart: 3, of which 1 were waited for; matrix products, arithmetic and copies ran while one was open for 0% of the time, Pallas kernels for 7%

profile of v2, /device:TPU:1, one launch (start us, length us, event | category | flops | bytes accessed | tf_op | source)
XLA Modules:
  0.0 139.5 jit_solution(12936220442562281122)
XLA Ops:
  0.6 0.0 copy-start
  0.6 0.0 copy-start.2
  0.7 1.9 %fusion = (f32[2,256,512]{2,1,0:T(8,128)S(1)}, f32[2,256,512]{2,1,0:T(8,128)S(1)}) fusion(f32[2,512,512]{2,1,0:T(8,128)} %obj_ref.1), kind=kLoop, calls=%fused_computation | loop fusion | bytes 4194304 | tf_op jit(solution)/shard_map/slice | solution.py:379
  2.5 0.0 copy-start.1
  2.5 0.0 copy-start.3
  2.6 0.0 copy-start.4
  2.6 0.0 copy-start.5
  2.6 1.6 %collective-permute-start.1 = (f32[2,256,512]{2,1,0:T(8,128)S(1)}, f32[2,256,512]{2,1,0:T(8,128)S(1)}, u32[]{:S(2)}, u32[]{:S(2)}) collective-permute-start(f32[2,256,512]{2,1,0:T(8,128)S(1)} %get-tuple-element.10), channel_id=1, source_target_pairs={{1,0},{2,1},{3,2},{5,4},{6,5},{7,6},{9,8},{10,9},{11,10},{13,12},{... | collective-permute-start | bytes 3145736 | tf_op jit(solution)/shard_map/ppermute | solution.py:220
  4.1 0.0 copy-done
  4.2 0.1 slice.15
  4.3 3.3 %collective-permute-start = (f32[2,512,256]{2,1,0:T(8,128)S(1)}, f32[2,512,256]{2,1,0:T(8,128)S(1)}, u32[]{:S(2)}, u32[]{:S(2)}) collective-permute-start(f32[2,512,256]{2,1,0:T(8,128)S(1)} %slice.15), channel_id=1, source_target_pairs={{4,0},{8,4},{12,8},{16,12},{20,16},{24,20},{28,24},{32,28},{36,32}... | collective-permute-start | bytes 3145736 | tf_op jit(solution)/shard_map/ppermute | solution.py:220
  8.2 21.2 %collective-permute-done.1.refs_2_ = f32[2,256,512]{2,1,0:T(8,128)S(1)} collective-permute-done((f32[2,256,512]{2,1,0:T(8,128)S(1)}, f32[2,256,512]{2,1,0:T(8,128)S(1)}, u32[]{:S(2)}, u32[]{:S(2)}) %collective-permute-start.1) | collective-permute-done | bytes 1048608 | tf_op jit(solution)/shard_map/ppermute | solution.py:220
  29.4 3.5 %collective-permute-start.2 = (f32[2,256,256]{2,1,0:T(8,128)S(1)}, f32[2,256,256]{2,1,0:T(8,128)S(1)}, u32[]{:S(2)}, u32[]{:S(2)}) collective-permute-start(f32[2,256,256]{2,1,0:T(8,128)S(1)} %slice.21), channel_id=1, source_target_pairs={{4,0},{8,4},{12,8},{16,12},{20,16},{24,20},{28,24},{32,28},{36,32}... | collective-permute-start | bytes 1572872 | tf_op jit(solution)/shard_map/ppermute | solution.py:220
  32.9 0.0 collective-permute-done.refs_1_
  32.9 0.0 copy-done.2
  32.9 0.0 copy-done.1
  33.0 0.0 copy-done.3
  33.0 0.0 copy-done.4
  33.0 0.0 copy-done.5
  33.0 0.0 copy-start.6
  33.0 1.0 copy-done.6
  34.0 0.9 copy-done.8
  35.0 0.9 copy-done.10
  35.9 10.1 %shard_map.113 = (f32[2,6,512,128]{3,2,1,0:T(8,128)S(1)}, f32[2,256,256]{2,1,0:T(8,128)S(1)}) custom-call(s32[1,1,32]{2,1,0:T(1,128)S(1)} %copy-done.3, s32[1,1,32]{2,1,0:T(1,128)S(1)} %copy-done.4, s32[1,1]{1,0:T(1,128)S(6)} %copy.14.count_ref, f32[2,256,256]{2,1,0:T(8,128)S(1)} %copy-done.1, bf16[1,1,32,256,256]{4,3,2,1,0:T(8,128)(2,1)S(1)} %copy-done.2, ...), custom_call_target="tpu_custom_call" | custom-call | flops 12000000000 | bytes 16000000 | tf_op jit(solution)/shard_map/pallas_call | solution.py:189
  46.1 0.0 collective-permute-done.2.refs_3_
  46.1 0.0 copy-done.7
  46.1 0.0 copy-done.9
  46.1 0.0 copy-done.11
  46.1 18.9 %shard_map.114 = (f32[2,6,512,128]{3,2,1,0:T(8,128)S(1)}, f32[2,256,256]{2,1,0:T(8,128)S(1)}) custom-call(s32[1,1,32]{2,1,0:T(1,128)S(1)} %copy-done.3, s32[1,1,32]{2,1,0:T(1,128)S(1)} %copy-done.4, s32[1,1]{1,0:T(1,128)S(6)} %copy.14.count_ref, f32[2,256,256]{2,1,0:T(8,128)S(1)} %copy-done.1, bf16[1,1,32,256,256]{4,3,2,1,0:T(8,128)(2,1)} %amp_ref.3, ...), custom_call_target="tpu_custom_call" | custom-call | flops 12000000000 | bytes 16000000 | tf_op jit(solution)/shard_map/pallas_call | solution.py:189
  65.1 72.3 %shard_map.115 = (f32[2,512,512]{2,1,0:T(8,128)S(1)}, f32[2,256,256]{2,1,0:T(8,128)S(1)}) custom-call(f32[2,6,512,128]{3,2,1,0:T(8,128)S(1)} %get-tuple-element.6.refs_4_.first_ref, f32[2,6,512,128]{3,2,1,0:T(8,128)S(1)} %get-tuple-element.8.second_ref, f32[2,512,512]{2,1,0:T(8,128)S(1)} %copy-done, f32[512,256]{1,0:T(8,128)S(1)} %bitcast.1, ...), custom_call_target="tpu_custom_call" | custom-call | tf_op jit(solution)/shard_map/pallas_call | solution.py:350
  137.4 1.3 copy.15
  138.7 0.8 copy.16
  (7 shorter events, 0.1 us)
Async XLA Ops:
  0.6 3.5 %copy-start = (f32[2,512,512]{2,1,0:T(8,128)S(1)}, f32[2,512,512]{2,1,0:T(8,128)}, u32[]{:S(2)}) copy-start(f32[2,512,512]{2,1,0:T(8,128)} %obj_ref.1) | copy-start | bytes 6291460
  0.6 32.3 %copy-start.2 = (bf16[1,1,32,256,256]{4,3,2,1,0:T(8,128)(2,1)S(1)}, bf16[1,1,32,256,256]{4,3,2,1,0:T(8,128)(2,1)}, u32[]{:S(2)}) copy-start(bf16[1,1,32,256,256]{4,3,2,1,0:T(8,128)(2,1)} %amp_ref.3) | copy-start | bytes 12582916
  2.5 30.4 %copy-start.1 = (f32[2,256,256]{2,1,0:T(8,128)S(1)}, f32[2,256,256]{2,1,0:T(8,128)}, u32[]{:S(2)}) copy-start(f32[2,256,256]{2,1,0:T(8,128)} %probe_ref.5) | copy-start | bytes 1572868
  2.5 30.4 %copy-start.3 = (s32[1,1,32]{2,1,0:T(1,128)S(1)}, s32[1,1,32]{2,1,0:T(1,128)}, u32[]{:S(2)}) copy-start(s32[1,1,32]{2,1,0:T(1,128)} %rows_ref.3) | copy-start | bytes 388
  2.6 30.4 %copy-start.4 = (s32[1,1,32]{2,1,0:T(1,128)S(1)}, s32[1,1,32]{2,1,0:T(1,128)}, u32[]{:S(2)}) copy-start(s32[1,1,32]{2,1,0:T(1,128)} %cols_ref.3) | copy-start | bytes 388
  2.6 30.4 %copy-start.5 = (bf16[512,512]{1,0:T(8,128)(2,1)S(1)}, bf16[512,512]{1,0:T(8,128)(2,1)}, u32[]{:S(2)}) copy-start(bf16[512,512]{1,0:T(8,128)(2,1)} %constant.11.clone.t4_ref) | copy-start | bytes 1572868
  2.6 26.8 %collective-permute-start.1 = (f32[2,256,512]{2,1,0:T(8,128)S(1)}, f32[2,256,512]{2,1,0:T(8,128)S(1)}, u32[]{:S(2)}, u32[]{:S(2)}) collective-permute-start(f32[2,256,512]{2,1,0:T(8,128)S(1)} %get-tuple-element.10), channel_id=1, source_target_pairs={{1,0},{2,1},{3,2},{5,4},{6,5},{7,6},{9,8},{10,9},{11,10},{13,12},{... | collective-permute-start | bytes 3145736 | tf_op jit(solution)/shard_map/ppermute | solution.py:220
  4.3 28.7 %collective-permute-start = (f32[2,512,256]{2,1,0:T(8,128)S(1)}, f32[2,512,256]{2,1,0:T(8,128)S(1)}, u32[]{:S(2)}, u32[]{:S(2)}) collective-permute-start(f32[2,512,256]{2,1,0:T(8,128)S(1)} %slice.15), channel_id=1, source_target_pairs={{4,0},{8,4},{12,8},{16,12},{20,16},{24,20},{28,24},{32,28},{36,32}... | collective-permute-start | bytes 3145736 | tf_op jit(solution)/shard_map/ppermute | solution.py:220
  29.4 16.7 %collective-permute-start.2 = (f32[2,256,256]{2,1,0:T(8,128)S(1)}, f32[2,256,256]{2,1,0:T(8,128)S(1)}, u32[]{:S(2)}, u32[]{:S(2)}) collective-permute-start(f32[2,256,256]{2,1,0:T(8,128)S(1)} %slice.21), channel_id=1, source_target_pairs={{4,0},{8,4},{12,8},{16,12},{20,16},{24,20},{28,24},{32,28},{36,32}... | collective-permute-start | bytes 1572872 | tf_op jit(solution)/shard_map/ppermute | solution.py:220
  33.0 1.0 copy-start.6
  34.0 0.9 copy-start.8
  35.0 0.9 copy-start.10
  35.9 10.2 %copy-start.7 = (bf16[512,512]{1,0:T(8,128)(2,1)S(1)}, bf16[512,512]{1,0:T(8,128)(2,1)}, u32[]{:S(2)}) copy-start(bf16[512,512]{1,0:T(8,128)(2,1)} %constant.9.clone.t2_ref) | copy-start | bytes 1572868
  35.9 10.2 %copy-start.9 = (bf16[2,256,256]{2,1,0:T(8,128)(2,1)S(1)}, bf16[2,256,256]{2,1,0:T(8,128)(2,1)}, u32[]{:S(2)}) copy-start(bf16[2,256,256]{2,1,0:T(8,128)(2,1)} %constant.10.clone.t3_ref) | copy-start | bytes 786436
  35.9 10.2 %copy-start.11 = (bf16[2,256,256]{2,1,0:T(8,128)(2,1)S(1)}, bf16[2,256,256]{2,1,0:T(8,128)(2,1)}, u32[]{:S(2)}) copy-start(bf16[2,256,256]{2,1,0:T(8,128)(2,1)} %constant.8.clone.t1_ref) | copy-start | bytes 786436
